TPU v7x, 128 devices: a whole 4x4x4 slice. The times are simulated.
128 devices in a mesh: rows: 32 (over x, z, core), modes: 4 (over y).
Axes of the slice: x: 4, y: 4, z: 4, core: 2. Of those that a mesh axis runs over, the one named last changes fastest.
Arguments:
- activations: bfloat16 [2048, 64, 2048], P('rows', None, 'modes'), may hold values from -6 to 6
- cotangent: bfloat16 [2048, 64, 2048], P('rows', None, 'modes'), may hold values from -6 to 6
- spectral_weight: bfloat16 [64, 64, 64, 128], P('rows', None, None, 'modes'), may hold values from -12 to 12
- linear_weight: bfloat16 [64, 64], replicated, may hold values from -0.75 to 0.75
- bias: float32 [64], replicated, may hold values from -4 to 4
Outputs:
- grad_input: bfloat16 [2048, 64, 2048], P('rows', None, 'modes')
- grad_spectral: float32 [64, 64, 64, 128], P('rows', None, None, 'modes')
- grad_linear: float32 [64, 64], replicated
- grad_bias: float32 [64], replicated
All inputs are finite; a program needn't handle non-finite values.
Results may differ from a plain program's by a relative error of at most 0.03.
Values may be sent and summed in bfloat16 or wider, within the bound.
A program may use at most 128 MiB of HBM per device.

v0:
```python
import math
import jax
import jax.numpy as jnp
from jax import lax
from jax.sharding import PartitionSpec as P

HIGHEST_PRECISION = lax.Precision.HIGHEST


def row_angles(freq_count, row_start, row_count, period):
    positions = jnp.arange(freq_count, dtype=jnp.int32)
    frequency = jnp.where(positions < freq_count // 2, positions, positions - freq_count)
    grid_rows = row_start + jnp.arange(row_count, dtype=jnp.int32)
    phases = frequency[:, None] * grid_rows[None, :] % period
    angles = phases.astype(jnp.float32) * (2.0 * math.pi / period)
    return (jnp.cos(angles), jnp.sin(angles))


def column_table(mode_count, col_start, col_count, period):
    mode_ids = jnp.arange(mode_count, dtype=jnp.int32)
    grid_cols = col_start + jnp.arange(col_count, dtype=jnp.int32)
    phases = grid_cols[:, None] * mode_ids[None, :] % period
    angles = phases.astype(jnp.float32) * (2.0 * math.pi / period)
    return jnp.stack([jnp.cos(angles), -jnp.sin(angles)], axis=-1).reshape(
        col_count, 2 * mode_count
    )


def column_weights(mode_count):
    mode_ids = jnp.arange(mode_count, dtype=jnp.int32)
    return jnp.repeat(jnp.where(mode_ids == 0, 1.0, 2.0).astype(jnp.float32), 2)


def to_freq(values, cos_rows, sin_rows):
    length = cos_rows.shape[0]
    stacked = jnp.concatenate([cos_rows, sin_rows], axis=0)
    product = jnp.dot(
        stacked,
        values.reshape(values.shape[0], -1),
        precision=HIGHEST_PRECISION,
        preferred_element_type=jnp.float32,
    )
    halves = product.reshape(2, length, values.shape[1], values.shape[2] // 2, 2)
    real_part = halves[0, ..., 0] + halves[1, ..., 1]
    imag_part = halves[0, ..., 1] - halves[1, ..., 0]
    return jnp.stack([real_part, imag_part], axis=-1).reshape(
        length, values.shape[1], values.shape[2]
    )


def to_rows(values, cos_cols, sin_cols):
    length = cos_cols.shape[0]
    stacked = jnp.concatenate([cos_cols, sin_cols], axis=0)
    product = jnp.dot(
        stacked, values.reshape(values.shape[0], -1), preferred_element_type=jnp.float32
    )
    halves = product.reshape(2, length, values.shape[1], values.shape[2] // 2, 2)
    real_part = halves[0, ..., 0] - halves[1, ..., 1]
    imag_part = halves[0, ..., 1] + halves[1, ..., 0]
    return jnp.stack([real_part, imag_part], axis=-1).reshape(
        length, values.shape[1], values.shape[2]
    )


def gelu_grad(preact):
    cumulative = 0.5 * (1.0 + jax.scipy.special.erf(preact * 0.7071067811865476))
    density = jnp.exp(-0.5 * preact * preact) * 0.3989422804014327
    return cumulative + preact * density


def body(activations, cotangent, spectral_weight, linear_weight, bias):
    rows_here, channels, cols_here = activations.shape
    row_devices = lax.axis_size("rows")
    mode_devices = lax.axis_size("modes")
    row_index = lax.axis_index("rows")
    mode_index = lax.axis_index("modes")
    grid_rows = rows_here * row_devices
    grid_cols = cols_here * mode_devices
    kept_rows = spectral_weight.shape[0]
    block_cols = spectral_weight.shape[3]
    freq_rows = kept_rows * row_devices
    spec_cols = block_cols * mode_devices
    inv_area = 1.0 / (grid_rows * grid_cols)
    forward_table = column_table(spec_cols // 2, mode_index * cols_here, cols_here, grid_cols)
    analysis = forward_table.astype(jnp.bfloat16)
    synthesis = (forward_table.T * column_weights(spec_cols // 2)[:, None]).astype(jnp.bfloat16)
    cos_rows, sin_rows = row_angles(freq_rows, row_index * rows_here, rows_here, grid_rows)
    cos_cols = cos_rows.T.astype(jnp.bfloat16)
    sin_cols = sin_rows.T.astype(jnp.bfloat16)

    def reduce_spectrum(term):
        arranged = term.reshape(row_devices, kept_rows, channels, mode_devices, block_cols)
        arranged = arranged.transpose(0, 3, 1, 2, 4).reshape(
            row_devices * mode_devices * kept_rows, channels, block_cols
        )
        return lax.psum_scatter(arranged, ("rows", "modes"), scatter_dimension=0, tiled=True)

    def expand_spectrum(spectrum):
        gathered = lax.all_gather(spectrum, ("rows", "modes"), axis=0, tiled=True)
        arranged = gathered.reshape(row_devices, mode_devices, kept_rows, channels, block_cols)
        arranged = arranged.transpose(0, 2, 3, 1, 4).reshape(freq_rows, channels, spec_cols)
        return to_rows(arranged, cos_cols, sin_cols).astype(jnp.bfloat16)

    partial_cols = jnp.einsum(
        "hcw,wq->hcq", activations, analysis, preferred_element_type=jnp.float32
    )
    spectrum = reduce_spectrum(to_freq(partial_cols, cos_rows, sin_rows)).astype(jnp.bfloat16)
    parts = spectrum.reshape(kept_rows, channels, block_cols // 2, 2)
    wparts = spectral_weight.reshape(kept_rows, channels, channels, block_cols // 2, 2)
    spec_re = parts[..., 0]
    spec_im = parts[..., 1]
    weight_re = wparts[..., 0]
    weight_im = wparts[..., 1]
    mixed_re = jnp.einsum(
        "kcm,kcom->kom", spec_re, weight_re, preferred_element_type=jnp.float32
    ) - jnp.einsum("kcm,kcom->kom", spec_im, weight_im, preferred_element_type=jnp.float32)
    mixed_im = jnp.einsum(
        "kcm,kcom->kom", spec_re, weight_im, preferred_element_type=jnp.float32
    ) + jnp.einsum("kcm,kcom->kom", spec_im, weight_re, preferred_element_type=jnp.float32)
    mixed = (
        jnp.stack([mixed_re, mixed_im], axis=-1)
        .reshape(kept_rows, channels, block_cols)
        .astype(jnp.bfloat16)
    )
    rowfield = expand_spectrum(mixed)
    spectral = (
        jnp.einsum("hcq,qw->hcw", rowfield, synthesis, preferred_element_type=jnp.float32)
        * inv_area
    )
    linear = jnp.einsum(
        "hcw,co->how", activations, linear_weight, preferred_element_type=jnp.float32
    )
    preact = spectral + linear + bias[None, :, None]
    dpre = (cotangent.astype(jnp.float32) * gelu_grad(preact)).astype(jnp.bfloat16)
    grad_lin_part = jnp.einsum("hcw,how->co", activations, dpre, preferred_element_type=jnp.float32)
    grad_bias_part = jnp.sum(dpre.astype(jnp.float32), axis=(0, 2))
    grad_lin_sum, grad_bias_sum = lax.psum((grad_lin_part, grad_bias_part), ("rows", "modes"))
    dpartial = (
        jnp.einsum("hcw,qw->hcq", dpre, synthesis, preferred_element_type=jnp.float32) * inv_area
    )
    dmixed = reduce_spectrum(to_freq(dpartial, cos_rows, sin_rows)).astype(jnp.bfloat16)
    dparts = dmixed.reshape(kept_rows, channels, block_cols // 2, 2)
    dmix_re = dparts[..., 0]
    dmix_im = dparts[..., 1]
    spec_re_wide = spec_re.astype(jnp.float32)
    spec_im_wide = spec_im.astype(jnp.float32)
    dmix_re_wide = dmix_re.astype(jnp.float32)
    dmix_im_wide = dmix_im.astype(jnp.float32)
    grad_real = (
        spec_re_wide[:, :, None, :] * dmix_re_wide[:, None, :, :]
        + spec_im_wide[:, :, None, :] * dmix_im_wide[:, None, :, :]
    )
    grad_imag = (
        spec_re_wide[:, :, None, :] * dmix_im_wide[:, None, :, :]
        - spec_im_wide[:, :, None, :] * dmix_re_wide[:, None, :, :]
    )
    grad_spectral = jnp.stack([grad_real, grad_imag], axis=-1).reshape(
        kept_rows, channels, channels, block_cols
    )
    dspec_re = jnp.einsum(
        "kcom,kom->kcm", weight_re, dmix_re, preferred_element_type=jnp.float32
    ) + jnp.einsum("kcom,kom->kcm", weight_im, dmix_im, preferred_element_type=jnp.float32)
    dspec_im = jnp.einsum(
        "kcom,kom->kcm", weight_re, dmix_im, preferred_element_type=jnp.float32
    ) - jnp.einsum("kcom,kom->kcm", weight_im, dmix_re, preferred_element_type=jnp.float32)
    dspectrum = (
        jnp.stack([dspec_re, dspec_im], axis=-1)
        .reshape(kept_rows, channels, block_cols)
        .astype(jnp.bfloat16)
    )
    drows = expand_spectrum(dspectrum)
    spectral_part = jnp.einsum("hcq,wq->hcw", drows, analysis, preferred_element_type=jnp.float32)
    local_part = jnp.einsum("how,co->hcw", dpre, linear_weight, preferred_element_type=jnp.float32)
    grad_input = (spectral_part + local_part).astype(jnp.bfloat16)
    return (grad_input, grad_spectral, grad_lin_sum / grid_rows, grad_bias_sum / grid_rows)


def solution(mesh):
    return jax.shard_map(
        body,
        mesh=mesh,
        in_specs=(
            P("rows", None, "modes"),
            P("rows", None, "modes"),
            P("rows", None, None, "modes"),
            P(),
            P(),
        ),
        out_specs=(P("rows", None, "modes"), P("rows", None, None, "modes"), P(), P()),
        check_vma=False,
    )
```

profile of v0, /device:TPU:1, one launch (start us, length us, event | category | flops | bytes accessed | tf_op | source)
XLA Modules:
  0.0 1558.9 jit_solution(16695946387777610892)
XLA Ops:
  7.3 0.5 fusion.58
  7.8 0.6 copy-done.3
  9.0 3.4 convolution_bitcast_fusion
  12.4 2.8 copy.152
  15.6 0.6 copy-done.8
  16.2 14.0 fusion.10
  30.2 0.6 fusion.23
  30.7 0.6 fusion.25
  31.3 2.5 pad_maximum_fusion
  33.8 7.2 copy.98
  41.0 4.9 copy.99
  46.0 1.1 copy-done.5
  47.2 0.4 copy.100
  47.6 636.6 %reduce-scatter.3.cloned.1.call-done = f32[2,64,32]{1,2,0:T(8,128)} async-done(((f32[256,64,32]{1,2,0:T(8,128)}), f32[2,64,32]{1,2,0:T(8,128)}) %reduce-scatter.3.cloned.1.call-update) | async-done | bytes 16400 | tf_op jit(solution)/shard_map/reduce_scatter | solution.py:96
  684.1 0.8 convert_element_type.104
  685.9 0.6 copy.103
  686.6 0.6 reduce-scatter.5.cloned.1.call-start
  687.2 0.7 mul.222
  687.9 0.6 pad_maximum_fusion.7
  688.5 67.7 %all-gather.3.cloned.1.call-done = bf16[256,64,32]{1,2,0:T(8,128)(2,1)} async-done(((bf16[2,64,32]{1,2,0:T(8,128)(2,1)}), bf16[256,64,32]{1,2,0:T(8,128)(2,1)}) %all-gather.3.cloned.1.call-update) | async-done | bytes 1048592 | tf_op jit(solution)/shard_map/all_gather | solution.py:99
  756.2 6.9 copy.104
  763.1 5.9 reshape_reshape.13
  769.0 1.1 copy.105
  770.1 2.9 fusion.28
  772.9 0.5 fusion.35
  773.4 0.5 fusion.36
  773.9 0.5 pad_maximum_fusion.2
  774.4 3.7 copy.109
  778.1 4.3 fusion.32
  782.5 6.0 convert_reduce_fusion
  788.5 2.0 copy-done.1
  790.5 1.3 convolution_multiply_fusion
  791.9 2.7 copy.158
  794.6 14.1 fusion.8
  808.7 0.6 fusion.17
  809.3 0.6 fusion.19
  809.8 2.4 pad_maximum_fusion.1
  812.3 7.3 copy.118
  819.6 4.8 copy.119
  824.5 0.6 copy-done.12
  825.4 4.8 convolution_bitcast_fusion.1
  830.1 64.0 %all-reduce = (f32[64,64]{0,1:T(8,128)S(1)}, f32[64]{0:T(128)S(1)}) all-reduce(f32[64,64]{0,1:T(8,128)S(1)} %convolution_bitcast_fusion.1, f32[64]{0:T(128)S(1)} %get-tuple-element.34), channel_id=1, replica_groups=mesh['rows'=32,'modes'=4] {'rows','modes'}, use_global_device_ids=true, to_apply=%region_2.3 | all-reduce | flops 4160 | bytes 33280 | tf_op jit(solution)/shard_map/psum | solution.py:137
  894.1 0.7 copy.129
  894.8 563.3 %reduce-scatter.5.cloned.1.call-done = f32[2,64,32]{1,2,0:T(8,128)} async-done(((f32[256,64,32]{1,2,0:T(8,128)}), f32[2,64,32]{1,2,0:T(8,128)}) %reduce-scatter.5.cloned.1.call-update) | async-done | bytes 16400 | tf_op jit(solution)/shard_map/reduce_scatter | solution.py:96
  1458.1 0.8 convert_element_type.109
  1458.9 0.4 fusion.43
  1459.2 0.4 fusion.39
  1459.6 0.4 fusion.44
  1460.0 0.4 fusion.40
  1460.4 0.6 copy.120
  1461.1 0.5 broadcast_multiply_fusion.1
  1461.6 6.7 fusion.67
  1468.4 5.0 multiply_add_fusion
  1473.3 3.6 pad_maximum_fusion.4
  1476.9 52.4 %all-gather.5.cloned.1.call-done = bf16[256,64,32]{1,2,0:T(8,128)(2,1)} async-done(((bf16[2,64,32]{1,2,0:T(8,128)(2,1)}), bf16[256,64,32]{1,2,0:T(8,128)(2,1)}) %all-gather.5.cloned.1.call-update) | async-done | bytes 1048592 | tf_op jit(solution)/shard_map/all_gather | solution.py:99
  1529.3 6.9 copy.121
  1536.2 5.9 reshape_reshape.15
  1542.1 1.3 copy.122
  1543.5 2.3 fusion.26
  1545.8 0.5 fusion.37
  1546.3 0.5 fusion.38
  1546.7 0.5 pad_maximum_fusion.3
  1547.2 0.7 slice-done.1
  1548.1 4.1 fusion.6
  (67 shorter events, 2.6 us)
Async XLA Ops:
  7.2 775.3 %copy-start = (bf16[64,64]{1,0:T(8,128)(2,1)S(1)}, bf16[64,64]{1,0:T(8,128)(2,1)}, u32[]{:S(2)}) copy-start(bf16[64,64]{1,0:T(8,128)(2,1)} %param.8) | copy-start | bytes 24580
  7.2 677.0 %reduce-scatter.3.cloned.1.call-start = ((), (), s32[]{:S(2)}) async-start(), calls=%async_computation.2 | async-start | bytes 4227072 | tf_op jit(solution)/shard_map/reduce_scatter | solution.py:96
  7.8 0.6 copy-start.3
  15.6 0.6 copy-start.8
  45.9 1.2 copy-start.5
  46.0 710.2 %all-gather.3.cloned.1.call-start = ((), (), s32[]{:S(2)}) async-start(), calls=%async_computation.3 | async-start | bytes 2113536 | tf_op jit(solution)/shard_map/all_gather | solution.py:99
  47.6 715.5 %copy-start.6 = (bf16[2,64,64,32]{2,1,3,0:T(8,128)(2,1)}, bf16[2,64,64,32]{2,1,3,0:T(8,128)(2,1)S(1)}, u32[]{:S(2)}) copy-start(bf16[2,64,64,32]{2,1,3,0:T(8,128)(2,1)S(1)} %copy.100) | copy-start | bytes 1572868
  684.9 78.2 %copy-start.11 = (bf16[2,64,32]{1,2,0:T(8,128)(2,1)}, bf16[2,64,32]{1,2,0:T(8,128)(2,1)S(1)}, u32[]{:S(2)}) copy-start(bf16[2,64,32]{1,2,0:T(8,128)(2,1)S(1)} %convert_element_type.104) | copy-start | bytes 24580
  686.6 771.5 %reduce-scatter.5.cloned.1.call-start = ((), (), s32[]{:S(2)}) async-start(), calls=%async_computation.4 | async-start | bytes 4227072 | tf_op jit(solution)/shard_map/reduce_scatter | solution.py:96
  773.9 4.2 copy-start.13
  778.1 4.3 copy-start.2
  778.1 4.4 copy-start.14
  778.1 4.4 copy-start.15
  788.5 2.0 copy-start.1
  791.9 2.7 copy-start.9
  824.4 0.7 copy-start.12
  824.4 704.9 %all-gather.5.cloned.1.call-start = ((), (), s32[]{:S(2)}) async-start(), calls=%async_computation.5 | async-start | bytes 2113536 | tf_op jit(solution)/shard_map/all_gather | solution.py:99
  825.3 633.5 %copy-start.7 = (bf16[2,64,64,32]{2,1,3,0:T(8,128)(2,1)S(1)}, bf16[2,64,64,32]{2,1,3,0:T(8,128)(2,1)}, u32[]{:S(2)}) copy-start(bf16[2,64,64,32]{2,1,3,0:T(8,128)(2,1)} %copy-done.6) | copy-start | bytes 1572868
  1536.2 7.2 copy-start.10
  1543.5 3.8 slice-start
  1545.8 2.2 slice-start.1
  1546.3 1.8 copy-start.4
Sparse Core Ops, SparseCore 0:
  46.1 638.0 reduce-scatter.2
  688.1 67.9 all-gather.2
  824.6 633.4 reduce-scatter.4
  1461.2 68.0 all-gather.4
where the time goes:
time: 1570 us; the launch traced here: 1560 us
  waiting for transfers between devices  1320 us (84%)
  local copies, waits for them, and re-layouts  71.3 us (5%)
  matrix products  66.3 us (4%)
  blocking collectives  64 us (4%)
  other arithmetic  22.1 us (1%)
    reduce_scatter x2, waiting for transfers between devices, reduce_spectrum(): lax.psum_scatter(arranged, ('rows', 'modes'), scatter_dimension=0, tiled=...  1200 us
    all_gather x2, waiting for transfers between devices, expand_spectrum(): gathered = lax.all_gather(spectrum, ('rows', 'modes'), axis=0, tiled=True)  120 us
    psum x1, blocking collectives, body(): lax.psum((grad_lin_part, grad_bias_part), ('rows', 'modes'))  64 us
  transfers between devices with their start and end apart: 4, of which 4 were waited for; matrix products, arithmetic and copies ran while one was open for 1% of the time, Pallas kernels for 0%

commit v1 on v0

--- a/solution.py
+++ b/solution.py
@@ -96,7 +96,12 @@
         return lax.psum_scatter(arranged, ("rows", "modes"), scatter_dimension=0, tiled=True)
 
     def expand_spectrum(spectrum):
-        gathered = lax.all_gather(spectrum, ("rows", "modes"), axis=0, tiled=True)
+        gathered = jnp.concatenate(
+            lax.all_to_all(
+                jnp.stack([spectrum] * lax.axis_size(("rows", "modes"))), ("rows", "modes"), 0, 0
+            ),
+            axis=0,
+        )
         arranged = gathered.reshape(row_devices, mode_devices, kept_rows, channels, block_cols)
         arranged = arranged.transpose(0, 2, 3, 1, 4).reshape(freq_rows, channels, spec_cols)
         return to_rows(arranged, cos_cols, sin_cols).astype(jnp.bfloat16)

time: 1570 us -> 1490 us (0.949)
  waiting for transfers between devices: 1320 us -> 1220 us
  starting transfers between devices: 0.69 us -> 24.9 us
    all_gather x2 -> x0, waiting for transfers between devices: 120 us -> none  [expand_spectrum(): gathered = lax.all_gather(spectrum, ('rows', 'modes'), axis=0, tiled=True)]
    all_to_all x0 -> x2, waiting for transfers between devices: none -> 29.1 us  [expand_spectrum(): lax.all_to_all(jnp.stack([spectrum] * lax.axis_size(('rows', 'modes'))),...]
    all_to_all x0 -> x2, starting transfers between devices: none -> 24.8 us  [expand_spectrum(): lax.all_to_all(jnp.stack([spectrum] * lax.axis_size(('rows', 'modes'))),...]
  transfers between devices with their start and end apart: 4 -> 4, of which waited for: 4 -> 4; matrix products, arithmetic and copies ran while one was open for 1% -> 2% of each run, Pallas kernels for 0% -> 0%
where the time goes in v1:
time: 1490 us
  waiting for transfers between devices  1220 us (82%)
  local copies, waits for them, and re-layouts  74.2 us (5%)
  matrix products  66.8 us (4%)
  blocking collectives  63.9 us (4%)
  starting transfers between devices  24.9 us (2%)
  other arithmetic  23.4 us (2%)
    reduce_scatter x2, waiting for transfers between devices, reduce_spectrum(): lax.psum_scatter(arranged, ('rows', 'modes'), scatter_dimension=0, tiled=...  1190 us
    psum x1, blocking collectives, body(): lax.psum((grad_lin_part, grad_bias_part), ('rows', 'modes'))  63.9 us
  transfers between devices with their start and end apart: 4, of which 4 were waited for; matrix products, arithmetic and copies ran while one was open for 2% of the time, Pallas kernels for 0%

profile of v1, /device:TPU:1, one launch (start us, length us, event | category | flops | bytes accessed | tf_op | source)
XLA Modules:
  0.0 1489.5 jit_solution(10514174604949095116)
XLA Ops:
  7.3 0.5 fusion.58
  7.8 0.6 copy-done.3
  9.0 3.4 convolution_bitcast_fusion
  12.4 3.0 copy.114
  15.4 0.8 fusion.71
  16.3 0.6 copy-done.8
  16.9 13.9 fusion.10
  30.8 0.6 fusion.23
  31.4 0.6 fusion.25
  31.9 2.5 pad_maximum_fusion
  34.4 7.3 copy.60
  41.7 4.9 copy.61
  46.6 1.2 copy-done.5
  48.2 638.2 %reduce-scatter.3.cloned.1.call-done = f32[2,64,32]{1,2,0:T(8,128)} async-done(((f32[256,64,32]{1,2,0:T(8,128)}), f32[2,64,32]{1,2,0:T(8,128)}) %reduce-scatter.3.cloned.1.call-update) | async-done | bytes 16400 | tf_op jit(solution)/shard_map/reduce_scatter | solution.py:96
  686.4 0.8 convert_element_type.108
  688.3 0.5 broadcast_bitcast_fusion.1
  688.8 2.3 reshape.407
  691.1 12.3 all-to-all-start
  703.5 0.7 mul.222
  704.2 1.3 pad_maximum_fusion.7
  705.5 17.8 %all-to-all-done = bf16[128,2,2048]{2,1,0:T(2,128)(2,1)S(1)} async-done(((bf16[128,2,2048]{2,1,0:T(2,128)(2,1)}), bf16[128,2,2048]{2,1,0:T(2,128)(2,1)S(1)}, u32[]{:S(2)}, u32[]{:S(2)}) %all-to-all-start) | async-done | bytes 1048608 | tf_op jit(solution)/shard_map/all_to_all | solution.py:100
  723.3 1.6 reshape.408
  724.9 4.6 copy.66
  729.5 5.9 reshape_reshape.20
  735.4 1.1 copy.67
  736.5 3.1 fusion.28
  739.6 0.5 fusion.35
  740.5 0.5 pad_maximum_fusion.2
  741.0 3.7 copy.71
  744.7 4.3 fusion.32
  749.1 6.0 convert_reduce_fusion
  755.1 2.0 copy-done.1
  757.1 1.3 convolution_multiply_fusion
  758.5 2.8 copy.120
  761.3 14.3 fusion.8
  775.6 0.6 fusion.17
  776.2 0.6 fusion.19
  776.7 2.5 pad_maximum_fusion.1
  779.2 7.2 copy.80
  786.5 5.0 copy.81
  791.5 0.7 copy-done.12
  792.4 4.7 convolution_bitcast_fusion.1
  797.1 63.9 %all-reduce = (f32[64,64]{0,1:T(8,128)S(1)}, f32[64]{0:T(128)S(1)}) all-reduce(f32[64,64]{0,1:T(8,128)S(1)} %convolution_bitcast_fusion.1, f32[64]{0:T(128)S(1)} %get-tuple-element.30), channel_id=1, replica_groups=mesh['rows'=32,'modes'=4] {'rows','modes'}, use_global_device_ids=true, to_apply=%region_2.3 | all-reduce | flops 4160 | bytes 33280 | tf_op jit(solution)/shard_map/psum | solution.py:142
  861.0 0.7 copy.91
  861.7 0.5 broadcast_multiply_fusion.1
  862.2 6.9 fusion.67
  869.0 554.2 %reduce-scatter.5.cloned.1.call-done = f32[2,64,32]{1,2,0:T(8,128)} async-done(((f32[256,64,32]{1,2,0:T(8,128)}), f32[2,64,32]{1,2,0:T(8,128)}) %reduce-scatter.5.cloned.1.call-update) | async-done | bytes 16400 | tf_op jit(solution)/shard_map/reduce_scatter | solution.py:96
  1423.2 0.8 convert_element_type.113
  1425.6 0.5 broadcast_bitcast_fusion
  1426.1 2.3 reshape.409
  1428.4 12.5 all-to-all-start.1
  1441.0 5.0 multiply_add_fusion
  1445.9 3.6 pad_maximum_fusion.4
  1449.5 11.3 all-to-all-done.1
  1460.8 1.4 reshape.410
  1462.2 4.6 copy.83
  1466.9 5.9 reshape_reshape.23
  1472.8 1.1 copy.84
  1473.9 2.3 fusion.26
  1476.2 0.5 fusion.37
  1476.6 0.5 fusion.38
  1477.1 0.5 pad_maximum_fusion.3
  1477.6 0.7 slice-done.1
  1478.4 4.1 fusion.6
  (71 shorter events, 4.6 us)
Async XLA Ops:
  7.2 741.9 %copy-start = (bf16[64,64]{1,0:T(8,128)(2,1)S(1)}, bf16[64,64]{1,0:T(8,128)(2,1)}, u32[]{:S(2)}) copy-start(bf16[64,64]{1,0:T(8,128)(2,1)} %param.8) | copy-start | bytes 24580
  7.2 679.3 %reduce-scatter.3.cloned.1.call-start = ((), (), s32[]{:S(2)}) async-start(), calls=%async_computation.4 | async-start | bytes 4227072 | tf_op jit(solution)/shard_map/reduce_scatter | solution.py:96
  7.8 0.7 copy-start.3
  16.2 0.6 copy-start.8
  46.6 1.2 copy-start.5
  48.2 640.0 %copy-start.6 = (bf16[2,64,64,32]{2,1,3,0:T(8,128)(2,1)}, bf16[2,64,64,32]{2,1,3,0:T(8,128)(2,1)S(1)}, u32[]{:S(2)}) copy-start(bf16[2,64,64,32]{2,1,3,0:T(8,128)(2,1)S(1)} %copy.62) | copy-start | bytes 1572868
  687.2 3.9 copy-start.11
  691.1 32.2 %all-to-all-start = ((bf16[128,2,2048]{2,1,0:T(2,128)(2,1)}), bf16[128,2,2048]{2,1,0:T(2,128)(2,1)S(1)}, u32[]{:S(2)}, u32[]{:S(2)}) async-start(bf16[128,2,2048]{2,1,0:T(2,128)(2,1)} %reshape.407), calls=%async_computation.1 | async-start | bytes 2097152 | tf_op jit(solution)/shard_map/all_to_all | solution.py:100
  703.4 719.8 %reduce-scatter.5.cloned.1.call-start = ((), (), s32[]{:S(2)}) async-start(), calls=%async_computation.5 | async-start | bytes 4227072 | tf_op jit(solution)/shard_map/reduce_scatter | solution.py:96
  740.5 4.2 copy-start.13
  744.7 4.3 copy-start.2
  744.7 4.3 copy-start.14
  744.7 4.4 copy-start.15
  755.1 2.0 copy-start.1
  758.5 2.8 copy-start.9
  791.4 0.7 copy-start.12
  862.2 561.8 %copy-start.7 = (bf16[2,64,64,32]{2,1,3,0:T(8,128)(2,1)S(1)}, bf16[2,64,64,32]{2,1,3,0:T(8,128)(2,1)}, u32[]{:S(2)}) copy-start(bf16[2,64,64,32]{2,1,3,0:T(8,128)(2,1)} %copy-done.6) | copy-start | bytes 1572868
  1428.4 32.4 %all-to-all-start.1 = ((bf16[128,2,2048]{2,1,0:T(2,128)(2,1)}), bf16[128,2,2048]{2,1,0:T(2,128)(2,1)S(1)}, u32[]{:S(2)}, u32[]{:S(2)}) async-start(bf16[128,2,2048]{2,1,0:T(2,128)(2,1)} %reshape.409), calls=%async_computation.3 | async-start | bytes 2097152 | tf_op jit(solution)/shard_map/all_to_all | solution.py:100
  1466.9 7.0 copy-start.10
  1473.8 3.8 slice-start
  1476.2 2.2 slice-start.1
  1476.6 1.8 copy-start.4
Sparse Core Ops, SparseCore 0:
  46.7 639.6 reduce-scatter.2
  791.6 631.5 reduce-scatter.4
